TPU v7x, 256 devices: a whole 4x4x8 slice. The times are simulated.
256 devices in a mesh: ctx: 16 (over z, y_hi), grp: 16 (over y_lo, x, core).
Axes of the slice: x: 4, y: 4 (y_hi: 2, y_lo: 2; y = y_hi * 2 + y_lo), z: 8, core: 2. Of those that a mesh axis runs over, the one named last changes fastest.
Arguments:
- q_latent: bfloat16 [4096, 1536], P('ctx'), may hold values from -210 to 210
- kv_latent: bfloat16 [4096, 576], P('ctx'), may hold values from -6 to 6
- kv_gain: float32 [512], replicated, may hold values from 0.1 to 1.9
- q_weight: bfloat16 [1536, 24576], P('ctx', 'grp'), may hold values from -0.15625 to 0.15625
- kv_weight: bfloat16 [512, 32768], P('ctx', 'grp'), may hold values from -0.25 to 0.25
- out_weight: bfloat16 [16384, 7168], P('grp', 'ctx'), may hold values from -0.0625 to 0.0625
- documents: int32 [4096], replicated, may hold values from 0 to 7, never falling along the last dimension, each value on 1 to 1024 neighbouring positions
Outputs:
- mixed: bfloat16 [4096, 7168], P('ctx', 'grp')
All inputs are finite; a program needn't handle non-finite values.
Results may differ from a plain program's by a relative error of at most 0.018.
Values may be sent and summed in bfloat16 or wider, within the bound.
A program may use at most 64 MiB of HBM per device.

v0:
```python
import jax
import jax.numpy as jnp
from jax import lax
from jax.sharding import Mesh
from jax.sharding import PartitionSpec as P

KL = 512
NOPE = 128
ROPE = 64
VDIM = 128
CTX = ("ctx_0", "ctx_1")
epsilon = 1e-06


def gather_axes(array, axes, dim):
    result = array
    for number in range(len(axes) - 1, -1, -1):
        result = lax.all_gather(result, axes[number], axis=dim, tiled=True)
    return result


def shifted(block, axis, distance):
    devices = range(lax.axis_size(axis))
    route = [(i - distance, i) for i in devices if i - distance in devices]
    return lax.ppermute(block, axis, route)


def joined_along(tiles, dim):
    lengths = list(tiles.shape[1:])
    lengths[dim] *= tiles.shape[0]
    return jnp.moveaxis(tiles, 0, dim).reshape(lengths)


def copy_for_each(array, axis):
    count = lax.axis_size(axis)
    return lax.all_to_all(
        jnp.broadcast_to(array[None], (count, *array.shape)), axis, 0, 0, tiled=True
    )


def gathered_copies(array, axis, dim):
    return joined_along(copy_for_each(array, axis), dim)


def in_blocks(array, dim, count):
    lengths = array.shape
    tiles = array.reshape(*lengths[:dim], count, lengths[dim] // count, *lengths[dim + 1 :])
    return jnp.moveaxis(tiles, dim, 0)


def summed_on_arrival(array, axis, dim):
    count = lax.axis_size(axis)
    tiles = lax.all_to_all(in_blocks(array, dim, count), axis, 0, 0, tiled=True)
    return jnp.sum(tiles.astype(jnp.float32), axis=0)


def rotate(inputs, positions):
    half_width = inputs.shape[-1] // 2
    inverse = 10000.0 ** (-2.0 * jnp.arange(half_width, dtype=jnp.float32) / inputs.shape[-1])
    angles = positions.astype(jnp.float32)[:, None] * inverse[None, :]
    shape = (angles.shape[0],) + (1,) * (inputs.ndim - 2) + (half_width,)
    cosine = jnp.cos(angles).reshape(shape)
    sine_part = jnp.sin(angles).reshape(shape)
    front_half = inputs[..., :half_width]
    back_half = inputs[..., half_width:]
    return jnp.concatenate(
        [front_half * cosine - back_half * sine_part, back_half * cosine + front_half * sine_part],
        axis=-1,
    )


def prepare(latent_block, positions, kv_gain):
    latent = latent_block[:, :KL].astype(jnp.float32)
    normed = (
        latent * lax.rsqrt(jnp.mean(latent * latent, axis=-1, keepdims=True) + epsilon) * kv_gain
    )
    key_rope = rotate(latent_block[:, KL:].astype(jnp.float32), positions).astype(jnp.bfloat16)
    return (normed.astype(jnp.bfloat16), key_rope)


def folder(left, weight_piece):
    return jnp.dot(left, weight_piece, preferred_element_type=jnp.float32)


def per_device(q_latent, kv_latent, kv_gain, q_weight, kv_weight, out_weight, documents):
    rows_dev = q_latent.shape[0]
    head_count = q_weight.shape[1] // (NOPE + ROPE)
    block_index = lax.axis_index(CTX)
    query_pos = block_index * rows_dev + jnp.arange(rows_dev, dtype=jnp.int32)
    prior_pos = query_pos - rows_dev
    query_full = folder(q_latent, gather_axes(q_weight, CTX, 0))
    query_full = query_full.reshape(rows_dev, head_count, NOPE + ROPE)
    query_nope = query_full[..., :NOPE].astype(jnp.bfloat16)
    query_rope = rotate(query_full[..., NOPE:], query_pos).astype(jnp.bfloat16)
    previous = shifted(kv_latent, CTX, 1)
    latent_block = jnp.concatenate([previous, kv_latent], axis=0)
    positions = jnp.concatenate([prior_pos, query_pos])
    normed, key_rope = prepare(latent_block, positions, kv_gain)
    key_value = folder(normed, gathered_copies(kv_weight, CTX, 0))
    key_value = key_value.astype(jnp.bfloat16)
    key_value = key_value.reshape(2 * rows_dev, head_count, NOPE + VDIM)
    key_nope = key_value[..., :NOPE]
    values = key_value[..., NOPE:]
    key_pos = jnp.concatenate([prior_pos, query_pos])
    query_docs = lax.dynamic_slice_in_dim(documents, block_index * rows_dev, rows_dev, 0)
    prior_docs = lax.dynamic_slice_in_dim(
        documents, jnp.maximum(block_index - 1, 0) * rows_dev, rows_dev, 0
    )
    key_docs = jnp.concatenate([prior_docs, query_docs])
    allowed = (
        (key_docs[None, :] == query_docs[:, None])
        & (key_pos[None, :] <= query_pos[:, None])
        & (key_pos[None, :] >= 0)
    )
    scale = (NOPE + ROPE) ** (-0.5)
    scores = jnp.einsum("qhd,khd->hqk", query_nope, key_nope, preferred_element_type=jnp.float32)
    scores = (
        scores + jnp.einsum("qhr,kr->hqk", query_rope, key_rope, preferred_element_type=jnp.float32)
    ) * scale
    scores = jnp.where(allowed[None], scores, -1e30)
    highest = jnp.max(scores, axis=-1, keepdims=True)
    weights = jnp.exp(scores - highest)
    probs = (weights / jnp.sum(weights, axis=-1, keepdims=True)).astype(jnp.bfloat16)
    attended = jnp.einsum("hqk,khv->qhv", probs, values, preferred_element_type=jnp.float32).astype(
        jnp.bfloat16
    )
    attended = attended.reshape(rows_dev, head_count * VDIM)
    partial_value = jnp.dot(
        attended,
        lax.all_gather(out_weight, CTX, axis=1, tiled=True),
        preferred_element_type=jnp.float32,
    )
    mixed = summed_on_arrival(partial_value.astype(jnp.bfloat16), "grp", 1).astype(jnp.bfloat16)
    return mixed


def solution(mesh):
    torus = Mesh(mesh.devices.reshape(8, 2, mesh.shape["grp"]), ("ctx_0", "ctx_1", "grp"))
    return jax.shard_map(
        per_device,
        mesh=torus,
        in_specs=(
            P(CTX, None),
            P(CTX, None),
            P(),
            P(CTX, "grp"),
            P(CTX, "grp"),
            P("grp", CTX),
            P(),
        ),
        out_specs=P(CTX, "grp"),
        check_vma=False,
    )
```

profile of v0, /device:TPU:1, one launch (start us, length us, event | category | flops | bytes accessed | tf_op | source)
XLA Modules:
  0.0 416.1 jit_solution(16607223282581625902)
XLA Ops:
  6.5 12.7 %all_gather.9 = bf16[192,1536]{1,0:T(8,128)(2,1)} all-gather(bf16[96,1536]{1,0:T(8,128)(2,1)} %param.10), channel_id=1, replica_groups=mesh['ctx_0'=8,'ctx_1'=2,'grp'=16] {'ctx_1'}, dimensions={0}, use_global_device_ids=true | all-gather | bytes 884736 | tf_op jit(solution)/shard_map/all_gather | solution.py:18
  19.3 0.0 all-gather.5.cloned.1.call-start
  19.3 0.7 all-gather.5.cloned.1.call-update
  20.0 2.5 broadcast_in_dim.10
  22.5 9.6 %all-to-all-start = ((bf16[16,32,2048]{2,1,0:T(8,128)(2,1)}), bf16[16,32,2048]{2,1,0:T(8,128)(2,1)S(1)}, u32[]{:S(2)}, u32[]{:S(2)}) async-start(bf16[16,32,2048]{2,1,0:T(8,128)(2,1)} %broadcast_in_dim.10), calls=%async_computation | async-start | bytes 4194304 | tf_op jit(solution)/shard_map/all_to_all | solution.py:36
  32.1 5.5 %collective-permute-start = (bf16[256,576]{0,1:T(8,128)(2,1)S(1)}, bf16[256,576]{0,1:T(8,128)(2,1)}, u32[]{:S(2)}, u32[]{:S(2)}) collective-permute-start(bf16[256,576]{0,1:T(8,128)(2,1)S(1)} %copy-done.3), channel_id=1, source_target_pairs={{0,16},{16,32},{32,48},{48,64},{64,80},{80,96},{96,112},{112,128},... | collective-permute-start | bytes 884744 | tf_op jit(solution)/shard_map/ppermute | solution.py:25
  37.6 0.8 fusion.34
  38.5 0.8 multiply_cosine_fusion.1
  39.3 0.8 and_and_fusion
  40.2 0.9 collective-permute-done
  41.0 1.0 constant_dynamic-update-slice_fusion.1
  42.0 1.0 constant_dynamic-update-slice_fusion
  43.0 0.2 fusion.5
  43.2 0.3 fusion.23
  43.5 59.8 %all-to-all-done = bf16[16,32,2048]{2,1,0:T(8,128)(2,1)S(1)} async-done(((bf16[16,32,2048]{2,1,0:T(8,128)(2,1)}), bf16[16,32,2048]{2,1,0:T(8,128)(2,1)S(1)}, u32[]{:S(2)}, u32[]{:S(2)}) %all-to-all-start) | async-done | bytes 2097184 | tf_op jit(solution)/shard_map/all_to_all | solution.py:36
  103.3 1.4 convolution_convert_fusion.1
  104.7 0.7 copy.31
  105.4 0.1 fusion.33
  105.6 20.3 %all-gather.3.cloned.1.call-done = bf16[1536,1536]{1,0:T(8,128)(2,1)} async-done(((bf16[192,1536]{1,0:T(8,128)(2,1)}), bf16[1536,1536]{1,0:T(8,128)(2,1)}) %all-gather.3.cloned.1.call-update) | async-done | bytes 4718608 | tf_op jit(solution)/shard_map/all_gather | solution.py:18
  125.9 4.3 %fusion.36 = f32[256,1536]{0,1:T(8,128)S(1)} fusion(bf16[256,1536]{1,0:T(8,128)(2,1)S(1)} %copy-done, bf16[1536,1536]{1,0:T(8,128)(2,1)} %all-gather.3.cloned.1.call-done), kind=kOutput, calls=%fused_computation.60 | convolution fusion | flops 1207959552 | bytes 7077888 | tf_op jit(solution)/shard_map/dot_general | solution.py:82
  130.2 0.1 subtract_convert_fusion
  130.3 0.8 fusion.8
  131.0 0.0 copy-done.2
  131.1 1.0 fusion.2
  132.0 2.0 copy-done.1
  134.0 1.7 fusion.35
  135.8 7.5 %fusion.4 = bf16[8,128,256]{2,1,0:T(8,128)(2,1)S(1)} fusion(f32[8,256]{1,0:T(8,128)S(1)} %fusion.35, bf16[512,8,128]{2,1,0:T(8,128)(2,1)S(1)} %get-tuple-element.5, f32[8,256,512]{2,1,0:T(8,128)} %copy-done.1), kind=kOutput, calls=%fused_computation.11 | convolution fusion | flops 271845888 | bytes 5775360 | tf_op jit(solution)/shard_map/hqk,khv->qhv/dot_general | solution.py:124
  143.3 191.3 %all-gather.5.cloned.1.call-done = bf16[1024,7168]{0,1:T(8,128)(2,1)} async-done(((bf16[1024,448]{0,1:T(8,128)(2,1)}), bf16[1024,7168]{0,1:T(8,128)(2,1)}) %all-gather.5.cloned.1.call-update) | async-done | bytes 14680080 | tf_op jit(solution)/shard_map/all_gather | solution.py:130
  334.6 16.4 %convolution_convert_fusion = bf16[256,7168]{1,0:T(8,128)(2,1)} fusion(bf16[256,1024]{0,1:T(8,128)(2,1)S(1)} %bitcast.32, bf16[1024,7168]{0,1:T(8,128)(2,1)} %all-gather.5.cloned.1.call-done), kind=kOutput, calls=%fused_computation.1 | convolution fusion | flops 3759931392 | bytes 18874368 | tf_op jit(solution)/shard_map/dot_general | solution.py:128
  351.0 5.9 %copy.25 = bf16[256,7168]{0,1:T(8,128)(2,1)} copy(bf16[256,7168]{1,0:T(8,128)(2,1)} %convolution_convert_fusion) | data formatting | bytes 7340032 | tf_op jit(solution)/shard_map/convert_element_type | solution.py:133
  356.9 49.1 %all_to_all.10 = bf16[16,256,448]{1,2,0:T(8,128)(2,1)} all-to-all(bf16[16,256,448]{1,2,0:T(8,128)(2,1)} %bitcast.26), channel_id=1, replica_groups=mesh['ctx_0'=8,'ctx_1'=2,'grp'=16] {'grp'}, dimensions={0} | all-to-all | bytes 7340032 | tf_op jit(solution)/shard_map/all_to_all | solution.py:53
  406.0 3.3 reduce_sum.32
  (22 shorter events, 0.1 us)
Async XLA Ops:
  6.5 119.3 %copy-start = (bf16[256,1536]{1,0:T(8,128)(2,1)S(1)}, bf16[256,1536]{1,0:T(8,128)(2,1)}, u32[]{:S(2)}) copy-start(bf16[256,1536]{1,0:T(8,128)(2,1)} %param.7) | copy-start | bytes 2359300
  6.5 25.5 %copy-start.3 = (bf16[256,576]{0,1:T(8,128)(2,1)S(1)}, bf16[256,576]{0,1:T(8,128)(2,1)}, u32[]{:S(2)}) copy-start(bf16[256,576]{0,1:T(8,128)(2,1)} %param.8) | copy-start | bytes 884740
  6.5 119.3 %all-gather.3.cloned.1.call-start = ((), (), s32[]{:S(2)}) async-start(), calls=%async_computation.2 | async-start | bytes 5308416 | tf_op jit(solution)/shard_map/all_gather | solution.py:18
  19.3 315.3 %all-gather.5.cloned.1.call-start = ((), (), s32[]{:S(2)}) async-start(), calls=%async_computation.3 | async-start | bytes 15597568 | tf_op jit(solution)/shard_map/all_gather | solution.py:130
  20.0 83.3 %copy-start.6 = (f32[512]{0:T(512)S(1)}, f32[512]{0:T(512)}, u32[]{:S(2)}) copy-start(f32[512]{0:T(512)} %param.9) | copy-start | bytes 6148
  22.5 80.8 %all-to-all-start = ((bf16[16,32,2048]{2,1,0:T(8,128)(2,1)}), bf16[16,32,2048]{2,1,0:T(8,128)(2,1)S(1)}, u32[]{:S(2)}, u32[]{:S(2)}) async-start(bf16[16,32,2048]{2,1,0:T(8,128)(2,1)} %broadcast_in_dim.10), calls=%async_computation | async-start | bytes 4194304 | tf_op jit(solution)/shard_map/all_to_all | solution.py:36
  32.1 9.0 %collective-permute-start = (bf16[256,576]{0,1:T(8,128)(2,1)S(1)}, bf16[256,576]{0,1:T(8,128)(2,1)}, u32[]{:S(2)}, u32[]{:S(2)}) collective-permute-start(bf16[256,576]{0,1:T(8,128)(2,1)S(1)} %copy-done.3), channel_id=1, source_target_pairs={{0,16},{16,32},{32,48},{48,64},{64,80},{80,96},{96,112},{112,128},... | collective-permute-start | bytes 884744 | tf_op jit(solution)/shard_map/ppermute | solution.py:25
  105.5 24.6 %copy-start.4 = (f32[256,32]{0,1:T(8,128)S(1)}, f32[256,32]{0,1:T(8,128)}, u32[]{:S(2)}) copy-start(f32[256,32]{0,1:T(8,128)} %get-tuple-element.15) | copy-start | bytes 98308
  105.6 24.6 %copy-start.5 = (f32[256,32]{0,1:T(8,128)S(1)}, f32[256,32]{0,1:T(8,128)}, u32[]{:S(2)}) copy-start(f32[256,32]{0,1:T(8,128)} %get-tuple-element.16) | copy-start | bytes 98308
  130.2 0.9 copy-start.2
  132.0 2.0 copy-start.1
Sparse Core Ops, SparseCore 0:
  19.4 106.4 all-gather.2
  128.5 206.0 all-gather.4
where the time goes:
time: 417 us; the launch traced here: 416 us
  waiting for transfers between devices  273 us (65%)
  blocking collectives  61.8 us (15%)
  matrix products  31.3 us (8%)
  starting transfers between devices  15.1 us (4%)
  local copies, waits for them, and re-layouts  14.1 us (3%)
  between operations  13.6 us (3%)
  other arithmetic  7.32 us (2%)
    all_gather x1, waiting for transfers between devices, per_device(): lax.all_gather(out_weight, CTX, axis=1, tiled=True)  191 us
    all_to_all x1, waiting for transfers between devices, copy_for_each(): lax.all_to_all(jnp.broadcast_to(array[None], (count, *array.shape)), axis...  59.8 us
    all_to_all x1, blocking collectives, summed_on_arrival(): tiles = lax.all_to_all(in_blocks(array, dim, count), axis, 0, 0, tiled=True)  49.1 us
    all_gather x1, waiting for transfers between devices, gather_axes(): result = lax.all_gather(result, axes[number], axis=dim, tiled=True)  20.3 us
    dot_general x1, matrix products, per_device(): jnp.dot(attended, lax.all_gather(out_weight, CTX, axis=1, tiled=True), pr...  16.4 us
    all_gather x1, blocking collectives, gather_axes(): result = lax.all_gather(result, axes[number], axis=dim, tiled=True)  12.7 us
    all_to_all x1, starting transfers between devices, copy_for_each(): lax.all_to_all(jnp.broadcast_to(array[None], (count, *array.shape)), axis...  9.55 us
  transfers between devices with their start and end apart: 4, of which 4 were waited for; matrix products, arithmetic and copies ran while one was open for 6% of the time, Pallas kernels for 0%

commit v1 on v0

--- a/solution.py
+++ b/solution.py
@@ -127,7 +127,9 @@
     attended = attended.reshape(rows_dev, head_count * VDIM)
     partial_value = jnp.dot(
         attended,
-        lax.all_gather(out_weight, CTX, axis=1, tiled=True),
+        jnp.concatenate(
+            lax.all_to_all(jnp.stack([out_weight] * lax.axis_size(CTX)), CTX, 0, 0), axis=1
+        ),
         preferred_element_type=jnp.float32,
     )
     mixed = summed_on_arrival(partial_value.astype(jnp.bfloat16), "grp", 1).astype(jnp.bfloat16)

time: 417 us -> 571 us (1.37)
  the two profiles are of different devices: /device:TPU:1 before, /device:TPU:96 now
where the time goes in v1:
time: 571 us; the launch traced here: 570 us
  waiting for transfers between devices  352 us (62%)
  blocking collectives  138 us (24%)
  matrix products  31.5 us (6%)
  local copies, waits for them, and re-layouts  20 us (4%)
  between operations  13.6 us (2%)
  starting transfers between devices  9.77 us (2%)
  other arithmetic  6.02 us (1%)
    ppermute x1, waiting for transfers between devices, shifted(): return lax.ppermute(block, axis, route)  352 us
    all_to_all x1, blocking collectives, copy_for_each(): lax.all_to_all(jnp.broadcast_to(array[None], (count, *array.shape)), axis...  60.4 us
    all_to_all x1, blocking collectives, summed_on_arrival(): tiles = lax.all_to_all(in_blocks(array, dim, count), axis, 0, 0, tiled=True)  49.3 us
    all_gather x1, blocking collectives, gather_axes(): result = lax.all_gather(result, axes[number], axis=dim, tiled=True)  27.8 us
    dot_general x1, matrix products, per_device(): jnp.dot(attended, jnp.concatenate(lax.all_to_all(jnp.stack([out_weight] *...  16.6 us
  transfers between devices with their start and end apart: 3, of which 1 were waited for; matrix products, arithmetic and copies ran while one was open for 4% of the time, Pallas kernels for 0%

profile of v1, /device:TPU:96, one launch (start us, length us, event | category | flops | bytes accessed | tf_op | source)
XLA Modules:
  0.0 570.3 jit_solution(8171488648848373302)
XLA Ops:
  6.5 1.2 broadcast_in_dim.10
  7.8 60.4 %all_to_all.15 = bf16[16,32,2048]{2,1,0:T(8,128)(2,1)S(1)} all-to-all(bf16[16,32,2048]{2,1,0:T(8,128)(2,1)S(1)} %broadcast_in_dim.10), channel_id=1, replica_groups=mesh['ctx_0'=8,'ctx_1'=2,'grp'=16] {'ctx_0','ctx_1'}, dimensions={0} | all-to-all | bytes 4194304 | tf_op jit(solution)/shard_map/all_to_all | solution.py:36
  68.2 8.2 %stack.2 = bf16[16,1024,448]{1,2,0:T(8,128)(2,1)} broadcast(bf16[1024,448]{0,1:T(8,128)(2,1)} %param.12), dimensions={1,2} | broadcast | bytes 15597568 | tf_op jit(solution)/shard_map/stack | solution.py:131
  76.5 7.1 %all-to-all-start.1 = ((bf16[16,1024,448]{1,2,0:T(8,128)(2,1)}), bf16[16,1024,448]{1,2,0:T(8,128)(2,1)}, u32[]{:S(2)}, u32[]{:S(2)}) async-start(bf16[16,1024,448]{1,2,0:T(8,128)(2,1)} %stack.2), calls=%async_computation.1 | async-start | bytes 29360128 | tf_op jit(solution)/shard_map/all_to_all | solution.py:131
  83.5 0.0 all-gather.2.cloned.1.call-start
  83.6 27.8 %all_gather.6 = bf16[192,1536]{1,0:T(8,128)(2,1)} all-gather(bf16[96,1536]{1,0:T(8,128)(2,1)S(1)} %copy-done.3), channel_id=1, replica_groups=mesh['ctx_0'=8,'ctx_1'=2,'grp'=16] {'ctx_1'}, dimensions={0}, use_global_device_ids=true | all-gather | bytes 884736 | tf_op jit(solution)/shard_map/all_gather | solution.py:18
  111.4 0.0 all-gather.2.cloned.1.call-update
  111.4 2.7 collective-permute-start
  114.1 0.8 fusion.34
  115.0 0.2 multiply_cosine_fusion.1
  115.2 0.2 and_and_fusion
  115.4 351.8 %collective-permute-done = bf16[256,576]{0,1:T(8,128)(2,1)} collective-permute-done((bf16[256,576]{0,1:T(8,128)(2,1)S(1)}, bf16[256,576]{0,1:T(8,128)(2,1)}, u32[]{:S(2)}, u32[]{:S(2)}) %collective-permute-start) | collective-permute-done | bytes 294944 | tf_op jit(solution)/shard_map/ppermute | solution.py:25
  467.2 1.0 constant_dynamic-update-slice_fusion.1
  468.2 0.2 fusion.5
  468.4 0.3 fusion.23
  468.7 0.0 copy-done.5
  468.7 1.4 convolution_convert_fusion.1
  470.1 0.7 copy.32
  470.8 0.1 fusion.33
  471.0 0.0 all-gather.2.cloned.1.call-done
  471.0 4.3 fusion.36
  475.3 0.1 subtract_convert_fusion
  475.4 0.8 fusion.8
  476.1 1.0 fusion.2
  477.1 1.9 copy-done.2
  479.0 1.7 fusion.35
  480.8 7.5 %fusion.4 = bf16[8,128,256]{2,1,0:T(8,128)(2,1)S(1)} fusion(f32[8,256]{1,0:T(8,128)S(1)} %fusion.35, bf16[512,8,128]{2,1,0:T(8,128)(2,1)S(1)} %get-tuple-element.5, f32[8,256,512]{2,1,0:T(8,128)} %copy-done.2), kind=kOutput, calls=%fused_computation.11 | convolution fusion | flops 271845888 | bytes 5775360 | tf_op jit(solution)/shard_map/hqk,khv->qhv/dot_general | solution.py:124
  488.3 0.0 all-to-all-done.1
  488.3 16.6 %convolution_convert_fusion = bf16[256,7168]{1,0:T(8,128)(2,1)} fusion(bf16[256,1024]{0,1:T(8,128)(2,1)S(1)} %bitcast.35, bf16[1024,7168]{0,1:T(8,128)(2,1)} %bitcast.7), kind=kOutput, calls=%fused_computation.1 | convolution fusion | flops 3759931392 | bytes 18874368 | tf_op jit(solution)/shard_map/dot_general | solution.py:128
  504.9 5.9 %copy.26 = bf16[256,7168]{0,1:T(8,128)(2,1)} copy(bf16[256,7168]{1,0:T(8,128)(2,1)} %convolution_convert_fusion) | data formatting | bytes 7340032 | tf_op jit(solution)/shard_map/convert_element_type | solution.py:135
  510.8 49.3 %all_to_all.16 = bf16[16,256,448]{1,2,0:T(8,128)(2,1)} all-to-all(bf16[16,256,448]{1,2,0:T(8,128)(2,1)} %bitcast.29), channel_id=1, replica_groups=mesh['ctx_0'=8,'ctx_1'=2,'grp'=16] {'grp'}, dimensions={0} | all-to-all | bytes 7340032 | tf_op jit(solution)/shard_map/all_to_all | solution.py:53
  560.1 3.3 reduce_sum.32
  (19 shorter events, 0.1 us)
Async XLA Ops:
  6.5 464.4 %copy-start = (bf16[256,1536]{1,0:T(8,128)(2,1)S(1)}, bf16[256,1536]{1,0:T(8,128)(2,1)}, u32[]{:S(2)}) copy-start(bf16[256,1536]{1,0:T(8,128)(2,1)} %param.7) | copy-start | bytes 2359300
  76.5 7.1 %copy-start.3 = (bf16[96,1536]{1,0:T(8,128)(2,1)S(1)}, bf16[96,1536]{1,0:T(8,128)(2,1)}, u32[]{:S(2)}) copy-start(bf16[96,1536]{1,0:T(8,128)(2,1)} %param.10) | copy-start | bytes 884740
  76.5 34.9 %copy-start.4 = (bf16[256,576]{0,1:T(8,128)(2,1)S(1)}, bf16[256,576]{0,1:T(8,128)(2,1)}, u32[]{:S(2)}) copy-start(bf16[256,576]{0,1:T(8,128)(2,1)} %param.8) | copy-start | bytes 884740
  76.5 392.3 %copy-start.5 = (f32[512]{0:T(512)S(1)}, f32[512]{0:T(512)}, u32[]{:S(2)}) copy-start(f32[512]{0:T(512)} %param.9) | copy-start | bytes 6148
  76.5 411.9 %all-to-all-start.1 = ((bf16[16,1024,448]{1,2,0:T(8,128)(2,1)}), bf16[16,1024,448]{1,2,0:T(8,128)(2,1)}, u32[]{:S(2)}, u32[]{:S(2)}) async-start(bf16[16,1024,448]{1,2,0:T(8,128)(2,1)} %stack.2), calls=%async_computation.1 | async-start | bytes 29360128 | tf_op jit(solution)/shard_map/all_to_all | solution.py:131
  83.5 387.5 %all-gather.2.cloned.1.call-start = ((), (), s32[]{:S(2)}) async-start(), calls=%async_computation.3 | async-start | bytes 5308416 | tf_op jit(solution)/shard_map/all_gather | solution.py:18
  111.4 355.8 %collective-permute-start = (bf16[256,576]{0,1:T(8,128)(2,1)S(1)}, bf16[256,576]{0,1:T(8,128)(2,1)}, u32[]{:S(2)}, u32[]{:S(2)}) collective-permute-start(bf16[256,576]{0,1:T(8,128)(2,1)S(1)} %copy-done.4), channel_id=1, source_target_pairs={{0,16},{16,32},{32,48},{48,64},{64,80},{80,96},{96,112},{112,128},... | collective-permute-start | bytes 884744 | tf_op jit(solution)/shard_map/ppermute | solution.py:25
  477.1 1.9 copy-start.2
  510.8 52.6 %copy-start.1 = (bf16[256,1536]{1,0:T(8,128)(2,1)S(1)}, bf16[256,1536]{1,0:T(8,128)(2,1)}, u32[]{:S(2)}) copy-start(bf16[256,1536]{1,0:T(8,128)(2,1)} %param.7) | copy-start | bytes 2359300
Sparse Core Ops, SparseCore 0:
  111.5 179.9 all-gather.1
